TPU v7x, 256 devices: a whole 4x4x8 slice. The times are simulated.
256 devices in a mesh: dp: 32 (over y, x, core), tensor: 8 (over z).
Axes of the slice: x: 4, y: 4, z: 8, core: 2. Of those that a mesh axis runs over, the one named last changes fastest.
Arguments:
- candidates: int32 [128, 16], P('dp'), may hold values from 0 to 63, all different within a row; in each aligned block of 4 rows (0 to 3, 4 to 7, ...) at most 2 rows name the same one
- sequence_place: int32 [64], replicated, may hold values from 0 to 63, each once
- activations: bfloat16 [64, 512, 28672], P('dp', None, 'tensor'), may hold values from -6 to 6
- gradients: bfloat16 [64, 512, 8192], P('dp', None, 'tensor'), may hold values from -6 to 6
- query_in: bfloat16 [128, 8, 28672], P('dp', None, 'tensor'), may hold values from -0.03125 to 0.03125
- query_out: bfloat16 [128, 8, 8192], P('dp', None, 'tensor'), may hold values from -0.0625 to 0.0625
Outputs:
- scores: float32 [128, 16, 512], P('dp', None, 'tensor')
Inputs may be any that keep to these rules, and one draw needn't show every extreme that they name: `candidates`: each row names 16 different sequences; within the rows of one device (aligned blocks of 4 rows) no sequence is named more than 2 times. Each sequence id appears once; sequence s is stored at row sequence_place[s] of activations and gradients.
All inputs are finite; a program needn't handle non-finite values.
Results may differ from a plain program's by a relative error of at most 0.0003.
Values may be sent and summed in bfloat16 or wider, within the bound.
No kernel may reach another device: no remote copies, remote signals or barrier semaphores. Data moves between devices by JAX's collectives and lax.ppermute only.
A program may use at most 192 MiB of HBM per device.

v0:
```python
import functools

import jax
import jax.numpy as jnp
from jax import lax
from jax.experimental import pallas as pl
from jax.experimental.pallas import tpu as pltpu
from jax.sharding import PartitionSpec as P


SIDE = 4


def place(y, x, core):
    return ((y % SIDE) * SIDE + x % SIDE) * 2 + core


def hop(phase, distance):
    pairs = []
    for y in range(SIDE):
        for x in range(SIDE):
            for core in range(2):
                along_x = (phase == 1) == (core == 0)
                dy, dx = (0, distance) if along_x else (distance, 0)
                pairs.append((place(y, x, core), place(y + dy, x + dx, core)))
    return pairs


PARTNER = [(i, i ^ 1) for i in range(2 * SIDE * SIDE)]
SAME_CORE = [[2 * chip + core for chip in range(SIDE * SIDE)] for core in range(2)]
OFFSETS = tuple((second, first) for first in (0, -1, 1, 2) for second in (0, -1, 1, 2))
HEAD = 19
MIB = 1024 * 1024
VMEM = pl.BlockSpec(memory_space=pltpu.VMEM)
SMEM = pl.BlockSpec(memory_space=pltpu.SMEM)
HBM = pl.BlockSpec(memory_space=pltpu.HBM)


def on_chip(arrays):
    return [pltpu.with_memory_space_constraint(a, pltpu.VMEM) for a in arrays]


def hold_kernel(info, *refs):
    count = len(refs) // 2
    sems = refs[-1]
    copies = [
        pltpu.make_async_copy(refs[i], refs[count + i], sems.at[i]) for i in range(count)
    ]
    for copy in copies:
        copy.start()
    for copy in copies:
        copy.wait()


def hold(info, *arrays):
    return pl.pallas_call(
        hold_kernel,
        in_specs=[SMEM] + [HBM] * len(arrays),
        out_specs=[VMEM] * len(arrays),
        out_shape=[jax.ShapeDtypeStruct(a.shape, a.dtype) for a in arrays],
        scratch_shapes=[pltpu.SemaphoreType.DMA((len(arrays),))],
        cost_estimate=pl.CostEstimate(
            flops=0, bytes_accessed=4 * sum(a.size for a in arrays), transcendentals=0
        ),
        compiler_params=pltpu.CompilerParams(vmem_limit_bytes=2 * MIB),
        name="hold",
    )(info, *[pltpu.with_memory_space_constraint(a, pltpu.HBM) for a in arrays])


def project_kernel(lengths, first, info, *refs):
    blocks, (acts, grads, part, own, plus, minus) = refs[:16], refs[16:22]
    table, table_scalars, sem, rows = refs[22], refs[23], refs[24], refs[25:27]
    in_width, out_width = acts.shape[-1], grads.shape[-1]
    shares, seqs = part.shape[0], part.shape[1]
    sources = table.shape[0]
    width = 16 * sources
    z, base = info[0], info[first]
    for n in range(sources):
        entry = blocks[n][0, :, in_width + out_width :].astype(jnp.float32)
        table[n : n + 1, :] = entry[0:1].astype(jnp.int32)
    copy = pltpu.make_async_copy(table, table_scalars, sem)
    copy.start()
    copy.wait()
    contract = (((1,), (1,)), ((), ()))
    for j in range(seqs):
        for m in range(2):
            for n in range(sources):
                query = table_scalars[n, m * 64 + base + j]
                rows[j][m * sources + n] = blocks[n][query]
    for j in range(seqs):
        chosen = rows[j][...].reshape(width, rows[j].shape[-1])
        side_in = lax.dot_general(
            acts[j], chosen[:, :in_width], contract, preferred_element_type=jnp.float32
        )
        side_out = lax.dot_general(
            grads[j],
            chosen[:, in_width : in_width + out_width],
            contract,
            preferred_element_type=jnp.float32,
        )
        part[:, j, :, :width] = side_in.reshape(shares, -1, width)
        part[:, j, :, width:] = side_out.reshape(shares, -1, width)
    own[...] = part[z]
    plus[...] = part[lax.rem(z + lengths[0], shares)]
    minus[...] = part[lax.rem(z + shares - lengths[1], shares)]


def project(info, first, blocks, acts, grads, shares, lengths):
    sources = 16
    seqs, tokens, in_width = acts.shape
    out_width = grads.shape[-1]
    row_width = blocks[0].shape[-1]
    share = (seqs, tokens // shares, sources * 32)
    return pl.pallas_call(
        functools.partial(project_kernel, lengths, first),
        in_specs=[SMEM] + [VMEM] * 18,
        out_specs=[VMEM] * 4,
        scratch_shapes=[
            pltpu.VMEM((sources, 128), jnp.int32),
            pltpu.SMEM((sources, 128), jnp.int32),
            pltpu.SemaphoreType.DMA,
        ]
        + [pltpu.VMEM((2 * sources, 8, row_width), jnp.bfloat16)] * 2,
        out_shape=[jax.ShapeDtypeStruct((shares, *share), jnp.float32)]
        + [jax.ShapeDtypeStruct(share, jnp.float32)] * 3,
        cost_estimate=pl.CostEstimate(
            flops=2 * seqs * tokens * sources * 16 * (in_width + out_width),
            bytes_accessed=seqs * (tokens + sources * 16) * (in_width + out_width) * 2,
            transcendentals=0,
        ),
        compiler_params=pltpu.CompilerParams(vmem_limit_bytes=18 * MIB),
        name="project",
    )(info, *on_chip((*blocks, acts, grads)))


def add_kernel(offsets, info, part, *refs):
    shares = part.shape[0]
    count = len(offsets)
    for offset, came, out in zip(offsets, refs[:count], refs[count:]):
        out[...] = came[...] + part[lax.rem(info[0] + offset + shares, shares)]


def add_shares(info, part, came, offsets):
    return pl.pallas_call(
        functools.partial(add_kernel, tuple(offsets)),
        in_specs=[SMEM] + [VMEM] * (1 + len(came)),
        out_specs=[VMEM] * len(came),
        out_shape=[jax.ShapeDtypeStruct(a.shape, a.dtype) for a in came],
        cost_estimate=pl.CostEstimate(
            flops=came[0].size * len(came), bytes_accessed=12 * came[0].size, transcendentals=0
        ),
        compiler_params=pltpu.CompilerParams(vmem_limit_bytes=2 * MIB),
        name="add_shares",
    )(info, *on_chip((part, *came)))


def score_kernel(info, *refs):
    out = refs[-1]
    for half in range(2):
        own, left, right = refs[3 * half : 3 * half + 3]
        for j in range(left.shape[0]):
            total = own[j] + left[j] + right[j]
            width = total.shape[-1] // 2
            product = total[:, :width] * total[:, width:]
            sources = width // 16
            ranked = product.T.reshape(2 * sources, 8, product.shape[0])
            summed = jnp.sum(ranked, axis=1)
            line = jnp.concatenate([summed[:sources], summed[sources:]], axis=1)
            for n in range(sources):
                out[info[3 + n], 2 * half + j, :] = line[n]


def score(info, terms):
    seqs, tokens, _ = terms[0].shape
    return pl.pallas_call(
        score_kernel,
        in_specs=[SMEM] + [VMEM] * 6,
        out_specs=VMEM,
        out_shape=jax.ShapeDtypeStruct((16, 2 * seqs, 2 * tokens), jnp.float32),
        compiler_params=pltpu.CompilerParams(vmem_limit_bytes=4 * MIB),
        name="score",
    )(info, *on_chip(terms))


def choose_kernel(where, returned, out):
    queries, count, tokens = out.shape
    for q in range(queries):
        for c in range(count):
            at = where[HEAD + q * count + c]
            line = returned[at // 2]
            slot = at % 2
            line = jnp.where(slot == 0, line[:tokens], line[tokens:])
            out[q, c, :] = line


def choose(where, returned, queries, count):
    _, width = returned.shape
    return pl.pallas_call(
        choose_kernel,
        in_specs=[SMEM, VMEM],
        out_specs=VMEM,
        out_shape=jax.ShapeDtypeStruct((queries, count, width // 2), jnp.float32),
        compiler_params=pltpu.CompilerParams(vmem_limit_bytes=4 * MIB),
        name="choose",
    )(where, *on_chip([returned]))


def local(candidates, sequence_place, activations, gradients, query_in, query_out):
    queries, count = candidates.shape
    total = sequence_place.shape[0]
    shares = lax.axis_size("tensor")
    device = lax.axis_index("dp")
    z = lax.axis_index("tensor")
    core = device % 2
    chip = device // 2

    other_acts = lax.ppermute(activations, "dp", PARTNER)
    other_grads = lax.ppermute(gradients, "dp", PARTNER)

    target_rows = jnp.take(sequence_place, candidates, axis=0)
    positions = jnp.arange(total, dtype=jnp.int32)
    listed = jnp.any(target_rows[:, :, None] == positions, axis=1)
    number = jnp.arange(queries, dtype=jnp.int32)[:, None]
    flags = listed.astype(jnp.int32)
    before = jnp.sum(
        jnp.where(number[:, :, None] > number[None, :, 0:1].reshape(1, queries, 1), flags[None], 0),
        axis=1,
    )
    slot_query = jnp.stack(
        [jnp.sum(jnp.where(listed & (before == m), number, 0), axis=0) for m in range(2)]
    )
    table = slot_query.reshape(1, 1, 2 * total).astype(jnp.bfloat16)
    block = jnp.concatenate(
        [query_in, query_out, jnp.broadcast_to(table, (queries, 8, 2 * total))], axis=-1
    )

    def dp(array, phase, distance):
        return lax.ppermute(array, "dp", hop(phase, distance))

    blocks = []
    lines = [("block", block), ("below", dp(block, 1, 1))]
    lines += [("above", dp(block, 1, -1)), ("far", dp(block, 1, 2))]
    for name, array in lines:
        up, down = dp(array, 2, 1), dp(array, 2, -1)
        on = dp(up, 2, 1) if name == "below" else dp(down, 2, -1)
        blocks += [array, up, down, on]

    offsets = jnp.array(OFFSETS, jnp.int32)
    y, x = chip // SIDE, chip % SIDE
    second_axis, first_axis = offsets[:, 0], offsets[:, 1]
    row = (y + jnp.where(core == 0, second_axis, first_axis)) % SIDE
    col = (x + jnp.where(core == 0, first_axis, second_axis)) % SIDE
    slot = jnp.sum(jnp.where(target_rows[:, :, None] == positions, before[:, None, :], 0), axis=2)
    kind = jnp.where((target_rows // 2) % 2 == core, 0, 2) + target_rows % 2
    where = ((target_rows // 4) * 4 + kind) * 2 + slot
    heads = jnp.stack([z, 2 * device, 2 * (device ^ 1)])
    info = jnp.concatenate([heads, row * SIDE + col, where.reshape(-1)]).astype(jnp.int32)

    ring = {1: [(i, (i + 1) % shares) for i in range(shares)]}
    ring[-1] = [(i, (i - 1) % shares) for i in range(shares)]

    def send(array, sign):
        return lax.ppermute(array, "tensor", ring[sign])

    held_a = hold(info, activations, gradients)
    held_b = (*hold(info, other_acts), other_grads)
    far_a, far_b = shares // 2, shares - 1 - shares // 2
    streams = []
    for base, held, lengths in ((1, held_a, (far_a, far_b)), (2, held_b, (far_b, far_a))):
        part, own, plus, minus = project(info, base, blocks, *held, shares, lengths)
        streams.append([own, send(plus, 1), send(minus, -1), part, lengths])
    for step in range(1, far_a):
        for stream in streams:
            _, plus, minus, part, lengths = stream
            came, signs = [], []
            for sign, array, length in ((1, plus, lengths[0]), (-1, minus, lengths[1])):
                if step < length:
                    came.append(array)
                    signs.append(sign)
            away = [s * (lengths[0 if s > 0 else 1] - step) for s in signs]
            sums = add_shares(info, part, came, away)
            for sign, total_so_far in zip(signs, sums):
                stream[1 if sign > 0 else 2] = send(total_so_far, sign)

    scores = score(info, [a for stream in streams for a in stream[:3]])
    returned = lax.all_to_all(
        scores, "dp", split_axis=0, concat_axis=0, tiled=True, axis_index_groups=SAME_CORE
    )

    return choose(info, returned.reshape(64, -1), queries, count)


def solution(mesh):
    return jax.shard_map(
        local,
        mesh=mesh,
        in_specs=(
            P("dp", None),
            P(),
            P("dp", None, "tensor"),
            P("dp", None, "tensor"),
            P("dp", None, "tensor"),
            P("dp", None, "tensor"),
        ),
        out_specs=P("dp", None, "tensor"),
        check_vma=False,
    )
```

profile of v0, /device:TPU:96, one launch (start us, length us, event | category | flops | bytes accessed | tf_op | source)
XLA Modules:
  0.0 126.2 jit_solution(11229383784184529232)
XLA Ops:
  2.7 2.8 %collective-permute-start.7 = (bf16[4,8,4736]{2,1,0:T(8,128)(2,1)S(1)}, bf16[4,8,4736]{2,1,0:T(8,128)(2,1)S(1)}, u32[]{:S(2)}, u32[]{:S(2)}) collective-permute-start(bf16[4,8,4736]{2,1,0:T(8,128)(2,1)S(1)} %maximum_maximum_fusion.refs_0_), channel_id=1, source_target_pairs={{0,48},{8,200},{16,0},{24,216},{32,16},{40,232},{48,32},{56,248},{... | collective-permute-start | bytes 909320 | tf_op jit(solution)/shard_map/ppermute | solution.py:238
  7.2 5.9 %collective-permute-done.7.refs_8_ = bf16[4,8,4736]{2,1,0:T(8,128)(2,1)S(1)} collective-permute-done((bf16[4,8,4736]{2,1,0:T(8,128)(2,1)S(1)}, bf16[4,8,4736]{2,1,0:T(8,128)(2,1)S(1)}, u32[]{:S(2)}, u32[]{:S(2)}) %collective-permute-start.7) | collective-permute-done | bytes 303136 | tf_op jit(solution)/shard_map/ppermute | solution.py:238
  13.2 3.0 %collective-permute-start.1 = (bf16[4,8,4736]{2,1,0:T(8,128)(2,1)S(1)}, bf16[4,8,4736]{2,1,0:T(8,128)(2,1)}, u32[]{:S(2)}, u32[]{:S(2)}) collective-permute-start(bf16[4,8,4736]{2,1,0:T(8,128)(2,1)S(1)} %maximum_maximum_fusion.refs_0_), channel_id=1, source_target_pairs={{0,192},{8,56},{16,208},{24,8},{32,224},{40,24},{48,240},{56,40},{... | collective-permute-start | bytes 909320 | tf_op jit(solution)/shard_map/ppermute | solution.py:238
  17.1 3.0 %collective-permute-start.9 = (bf16[4,8,4736]{2,1,0:T(8,128)(2,1)S(1)}, bf16[4,8,4736]{2,1,0:T(8,128)(2,1)S(1)}, u32[]{:S(2)}, u32[]{:S(2)}) collective-permute-start(bf16[4,8,4736]{2,1,0:T(8,128)(2,1)S(1)} %collective-permute-done.7.refs_8_), channel_id=1, source_target_pairs={{0,192},{8,56},{16,208},{24,8},{32,224},{40,24},{48,240},{56,40},{... | collective-permute-start | bytes 909320 | tf_op jit(solution)/shard_map/ppermute | solution.py:238
  20.5 3.8 %collective-permute-start.13 = (bf16[4,8,4736]{2,1,0:T(8,128)(2,1)S(1)}, bf16[4,8,4736]{2,1,0:T(8,128)(2,1)S(1)}, u32[]{:S(2)}, u32[]{:S(2)}) collective-permute-start(bf16[4,8,4736]{2,1,0:T(8,128)(2,1)S(1)} %collective-permute-done.11.refs_12_), channel_id=1, source_target_pairs={{0,192},{8,56},{16,208},{24,8},{32,224},{40,24},{48,240},{56,40},{... | collective-permute-start | bytes 909320 | tf_op jit(solution)/shard_map/ppermute | solution.py:238
  28.6 3.7 %collective-permute-start.5 = (bf16[4,8,4736]{2,1,0:T(8,128)(2,1)S(1)}, bf16[4,8,4736]{2,1,0:T(8,128)(2,1)}, u32[]{:S(2)}, u32[]{:S(2)}) collective-permute-start(bf16[4,8,4736]{2,1,0:T(8,128)(2,1)S(1)} %collective-permute-done.3.refs_4_), channel_id=1, source_target_pairs={{0,192},{8,56},{16,208},{24,8},{32,224},{40,24},{48,240},{56,40},{... | collective-permute-start | bytes 909320 | tf_op jit(solution)/shard_map/ppermute | solution.py:238
  33.1 3.2 %collective-permute-done.12.refs_13_ = bf16[4,8,4736]{2,1,0:T(8,128)(2,1)S(1)} collective-permute-done((bf16[4,8,4736]{2,1,0:T(8,128)(2,1)S(1)}, bf16[4,8,4736]{2,1,0:T(8,128)(2,1)S(1)}, u32[]{:S(2)}, u32[]{:S(2)}) %collective-permute-start.12) | collective-permute-done | bytes 303136 | tf_op jit(solution)/shard_map/ppermute | solution.py:238
  37.4 3.0 %collective-permute-start.10 = (bf16[4,8,4736]{2,1,0:T(8,128)(2,1)}, bf16[4,8,4736]{2,1,0:T(8,128)(2,1)}, u32[]{:S(2)}, u32[]{:S(2)}) collective-permute-start(bf16[4,8,4736]{2,1,0:T(8,128)(2,1)} %copy-done.3), channel_id=1, source_target_pairs={{0,192},{8,56},{16,208},{24,8},{32,224},{40,24},{48,240},{56,40},{... | collective-permute-start | bytes 909320 | tf_op jit(solution)/shard_map/ppermute | solution.py:238
  41.2 3.0 %collective-permute-done.2.refs_3_ = bf16[4,8,4736]{2,1,0:T(8,128)(2,1)} collective-permute-done((bf16[4,8,4736]{2,1,0:T(8,128)(2,1)}, bf16[4,8,4736]{2,1,0:T(8,128)(2,1)}, u32[]{:S(2)}, u32[]{:S(2)}) %collective-permute-start.2) | collective-permute-done | bytes 303136 | tf_op jit(solution)/shard_map/ppermute | solution.py:238
  44.4 4.2 %hold.2 = (bf16[2,512,3584]{2,1,0:T(8,128)(2,1)S(1)}, bf16[2,512,1024]{2,1,0:T(8,128)(2,1)S(1)}) custom-call(s32[83]{0:T(128)S(1)} %concatenate.6.info.where, bf16[2,512,3584]{2,1,0:T(8,128)(2,1)} %refs_0_.1, bf16[2,512,1024]{2,1,0:T(8,128)(2,1)} %refs_1_.1), custom_call_target="tpu_custom_call" | custom-call | bytes 18874368 | tf_op jit(solution)/shard_map/hold/pallas_call | solution.py:56
  52.5 4.9 %project.2 = (f32[8,2,64,512]{3,2,1,0:T(8,128)S(1)}, f32[2,64,512]{2,1,0:T(8,128)S(1)}, f32[2,64,512]{2,1,0:T(8,128)S(1)}, f32[2,64,512]{2,1,0:T(8,128)S(1)}) custom-call(s32[83]{0:T(128)S(1)} %concatenate.6.info.where, bf16[4,8,4736]{2,1,0:T(8,128)(2,1)S(1)} %maximum_maximum_fusion.refs_0_, bf16[4,8,4736]{2,1,0:T(8,128)(2,1)S(1)} %copy-done.2, ...), custom_call_target="tpu_custom_call" | custom-call | flops 2415919104 | bytes 14155776 | tf_op jit(solution)/shard_map/project/pallas_call | solution.py:114
  57.5 3.2 %collective-permute-start.15 = (f32[2,64,512]{2,1,0:T(8,128)S(1)}, f32[2,64,512]{2,1,0:T(8,128)S(1)}, u32[]{:S(2)}, u32[]{:S(2)}) collective-permute-start(f32[2,64,512]{2,1,0:T(8,128)S(1)} %get-tuple-element.27), channel_id=1, source_target_pairs={{0,1},{1,2},{2,3},{3,4},{4,5},{5,6},{6,7},{7,0},{8,9},{9,10},{10,1... | collective-permute-start | bytes 786440 | tf_op jit(solution)/shard_map/ppermute | solution.py:263
  60.7 3.6 %hold.3.refs_16_ = bf16[2,512,3584]{2,1,0:T(8,128)(2,1)S(1)} custom-call(s32[83]{0:T(128)S(1)} %concatenate.6.info.where, bf16[2,512,3584]{2,1,0:T(8,128)(2,1)} %collective-permute-done.22.refs_0_), custom_call_target="tpu_custom_call" | custom-call | bytes 14680064 | tf_op jit(solution)/shard_map/hold/pallas_call | solution.py:56
  64.3 4.9 %project.3 = (f32[8,2,64,512]{3,2,1,0:T(8,128)S(1)}, f32[2,64,512]{2,1,0:T(8,128)S(1)}, f32[2,64,512]{2,1,0:T(8,128)S(1)}, f32[2,64,512]{2,1,0:T(8,128)S(1)}) custom-call(s32[83]{0:T(128)S(1)} %concatenate.6.info.where, bf16[4,8,4736]{2,1,0:T(8,128)(2,1)S(1)} %maximum_maximum_fusion.refs_0_, bf16[4,8,4736]{2,1,0:T(8,128)(2,1)S(1)} %copy-done.2, ...), custom_call_target="tpu_custom_call" | custom-call | flops 2415919104 | bytes 14155776 | tf_op jit(solution)/shard_map/project/pallas_call | solution.py:114
  69.3 3.3 %collective-permute-start.24 = (f32[2,64,512]{2,1,0:T(8,128)S(1)}, f32[2,64,512]{2,1,0:T(8,128)S(1)}, u32[]{:S(2)}, u32[]{:S(2)}) collective-permute-start(f32[2,64,512]{2,1,0:T(8,128)S(1)} %get-tuple-element.35), channel_id=1, source_target_pairs={{0,1},{1,2},{2,3},{3,4},{4,5},{5,6},{6,7},{7,0},{8,9},{9,10},{10,1... | collective-permute-start | bytes 786440 | tf_op jit(solution)/shard_map/ppermute | solution.py:263
  73.2 3.3 %collective-permute-start.17 = (f32[2,64,512]{2,1,0:T(8,128)S(1)}, f32[2,64,512]{2,1,0:T(8,128)S(1)}, u32[]{:S(2)}, u32[]{:S(2)}) collective-permute-start(f32[2,64,512]{2,1,0:T(8,128)S(1)} %get-tuple-element.29), channel_id=1, source_target_pairs={{0,1},{1,2},{2,3},{3,4},{4,5},{5,6},{6,7},{7,0},{8,9},{9,10},{10,1... | collective-permute-start | bytes 786440 | tf_op jit(solution)/shard_map/ppermute | solution.py:263
  78.6 3.9 %collective-permute-done.25.refs_1_ = f32[2,64,512]{2,1,0:T(8,128)S(1)} collective-permute-done((f32[2,64,512]{2,1,0:T(8,128)S(1)}, f32[2,64,512]{2,1,0:T(8,128)S(1)}, u32[]{:S(2)}, u32[]{:S(2)}) %collective-permute-start.25) | collective-permute-done | bytes 262176 | tf_op jit(solution)/shard_map/ppermute | solution.py:263
  86.4 2.2 %collective-permute-start.19 = (f32[2,64,512]{2,1,0:T(8,128)S(1)}, f32[2,64,512]{2,1,0:T(8,128)S(1)}, u32[]{:S(2)}, u32[]{:S(2)}) collective-permute-start(f32[2,64,512]{2,1,0:T(8,128)S(1)} %get-tuple-element.31), channel_id=1, source_target_pairs={{0,1},{1,2},{2,3},{3,4},{4,5},{5,6},{6,7},{7,0},{8,9},{9,10},{10,1... | collective-permute-start | bytes 786440 | tf_op jit(solution)/shard_map/ppermute | solution.py:263
  90.1 3.2 %collective-permute-done.27.refs_1_ = f32[2,64,512]{2,1,0:T(8,128)S(1)} collective-permute-done((f32[2,64,512]{2,1,0:T(8,128)S(1)}, f32[2,64,512]{2,1,0:T(8,128)S(1)}, u32[]{:S(2)}, u32[]{:S(2)}) %collective-permute-start.27) | collective-permute-done | bytes 262176 | tf_op jit(solution)/shard_map/ppermute | solution.py:263
  96.3 2.9 %collective-permute-start.20 = (f32[2,64,512]{2,1,0:T(8,128)S(1)}, f32[2,64,512]{2,1,0:T(8,128)S(1)}, u32[]{:S(2)}, u32[]{:S(2)}) collective-permute-start(f32[2,64,512]{2,1,0:T(8,128)S(1)} %add_shares.8), channel_id=1, source_target_pairs={{0,1},{1,2},{2,3},{3,4},{4,5},{5,6},{6,7},{7,0},{8,9},{9,10},{10,1... | collective-permute-start | bytes 786440 | tf_op jit(solution)/shard_map/ppermute | solution.py:263
  100.1 3.4 %collective-permute-done.29.refs_0_ = f32[2,64,512]{2,1,0:T(8,128)S(1)} collective-permute-done((f32[2,64,512]{2,1,0:T(8,128)S(1)}, f32[2,64,512]{2,1,0:T(8,128)S(1)}, u32[]{:S(2)}, u32[]{:S(2)}) %collective-permute-start.29) | collective-permute-done | bytes 262176 | tf_op jit(solution)/shard_map/ppermute | solution.py:263
  104.2 2.1 %collective-permute-done.21.refs_2_ = f32[2,64,512]{2,1,0:T(8,128)S(1)} collective-permute-done((f32[2,64,512]{2,1,0:T(8,128)S(1)}, f32[2,64,512]{2,1,0:T(8,128)S(1)}, u32[]{:S(2)}, u32[]{:S(2)}) %collective-permute-start.21) | collective-permute-done | bytes 262176 | tf_op jit(solution)/shard_map/ppermute | solution.py:263
  106.3 5.4 %collective-permute-done.30.refs_5_ = f32[2,64,512]{2,1,0:T(8,128)S(1)} collective-permute-done((f32[2,64,512]{2,1,0:T(8,128)S(1)}, f32[2,64,512]{2,1,0:T(8,128)S(1)}, u32[]{:S(2)}, u32[]{:S(2)}) %collective-permute-start.30) | collective-permute-done | bytes 262176 | tf_op jit(solution)/shard_map/ppermute | solution.py:263
  112.7 11.8 %all_to_all.5 = f32[16,4,128]{2,1,0:T(4,128)S(1)} all-to-all(f32[16,4,128]{2,1,0:T(4,128)S(1)} %score.1), channel_id=1, replica_groups={{0,16,32,48,64,80,96,112,128,144,160,176,192,208,224,240},{8,24,40,56,7..., dimensions={0} | all-to-all | bytes 65536 | tf_op jit(solution)/shard_map/all_to_all | solution.py:286
  (105 shorter events, 31.8 us)
Async XLA Ops:
  0.0 60.6 %collective-permute-start.22 = (bf16[2,512,3584]{2,1,0:T(8,128)(2,1)}, bf16[2,512,3584]{2,1,0:T(8,128)(2,1)}, u32[]{:S(2)}, u32[]{:S(2)}) collective-permute-start(bf16[2,512,3584]{2,1,0:T(8,128)(2,1)} %refs_0_.1), channel_id=1, source_target_pairs={{0,8},{8,0},{16,24},{24,16},{32,40},{40,32},{48,56},{56,48},{64,72... | collective-permute-start | bytes 22020104 | tf_op jit(solution)/shard_map/ppermute | solution.py:217
  0.1 64.2 %collective-permute-start.23 = (bf16[2,512,1024]{2,1,0:T(8,128)(2,1)}, bf16[2,512,1024]{2,1,0:T(8,128)(2,1)S(1)}, u32[]{:S(2)}, u32[]{:S(2)}) collective-permute-start(bf16[2,512,1024]{2,1,0:T(8,128)(2,1)} %refs_1_.1), channel_id=1, source_target_pairs={{0,8},{8,0},{16,24},{24,16},{32,40},{40,32},{48,56},{56,48},{64,72... | collective-permute-start | bytes 6291464 | tf_op jit(solution)/shard_map/ppermute | solution.py:218
  2.7 10.4 %collective-permute-start.7 = (bf16[4,8,4736]{2,1,0:T(8,128)(2,1)S(1)}, bf16[4,8,4736]{2,1,0:T(8,128)(2,1)S(1)}, u32[]{:S(2)}, u32[]{:S(2)}) collective-permute-start(bf16[4,8,4736]{2,1,0:T(8,128)(2,1)S(1)} %maximum_maximum_fusion.refs_0_), channel_id=1, source_target_pairs={{0,48},{8,200},{16,0},{24,216},{32,16},{40,232},{48,32},{56,248},{... | collective-permute-start | bytes 909320 | tf_op jit(solution)/shard_map/ppermute | solution.py:238
  5.6 10.6 %collective-permute-start.11 = (bf16[4,8,4736]{2,1,0:T(8,128)(2,1)S(1)}, bf16[4,8,4736]{2,1,0:T(8,128)(2,1)S(1)}, u32[]{:S(2)}, u32[]{:S(2)}) collective-permute-start(bf16[4,8,4736]{2,1,0:T(8,128)(2,1)S(1)} %maximum_maximum_fusion.refs_0_), channel_id=1, source_target_pairs={{0,32},{8,136},{16,48},{24,152},{32,0},{40,168},{48,16},{56,184},{... | collective-permute-start | bytes 909320 | tf_op jit(solution)/shard_map/ppermute | solution.py:238
  6.4 10.8 %collective-permute-start.3 = (bf16[4,8,4736]{2,1,0:T(8,128)(2,1)S(1)}, bf16[4,8,4736]{2,1,0:T(8,128)(2,1)S(1)}, u32[]{:S(2)}, u32[]{:S(2)}) collective-permute-start(bf16[4,8,4736]{2,1,0:T(8,128)(2,1)S(1)} %maximum_maximum_fusion.refs_0_), channel_id=1, source_target_pairs={{0,16},{8,72},{16,32},{24,88},{32,48},{40,104},{48,0},{56,120},{64... | collective-permute-start | bytes 909320 | tf_op jit(solution)/shard_map/ppermute | solution.py:238
  16.2 8.1 %collective-permute-start = (bf16[4,8,4736]{2,1,0:T(8,128)(2,1)S(1)}, bf16[4,8,4736]{2,1,0:T(8,128)(2,1)S(1)}, u32[]{:S(2)}, u32[]{:S(2)}) collective-permute-start(bf16[4,8,4736]{2,1,0:T(8,128)(2,1)S(1)} %maximum_maximum_fusion.refs_0_), channel_id=1, source_target_pairs={{0,64},{8,24},{16,80},{24,40},{32,96},{40,56},{48,112},{56,8},{64,... | collective-permute-start | bytes 909320 | tf_op jit(solution)/shard_map/ppermute | solution.py:238
  20.5 8.1 %collective-permute-start.13 = (bf16[4,8,4736]{2,1,0:T(8,128)(2,1)S(1)}, bf16[4,8,4736]{2,1,0:T(8,128)(2,1)S(1)}, u32[]{:S(2)}, u32[]{:S(2)}) collective-permute-start(bf16[4,8,4736]{2,1,0:T(8,128)(2,1)S(1)} %collective-permute-done.11.refs_12_), channel_id=1, source_target_pairs={{0,192},{8,56},{16,208},{24,8},{32,224},{40,24},{48,240},{56,40},{... | collective-permute-start | bytes 909320 | tf_op jit(solution)/shard_map/ppermute | solution.py:238
  25.0 11.3 %collective-permute-start.12 = (bf16[4,8,4736]{2,1,0:T(8,128)(2,1)S(1)}, bf16[4,8,4736]{2,1,0:T(8,128)(2,1)S(1)}, u32[]{:S(2)}, u32[]{:S(2)}) collective-permute-start(bf16[4,8,4736]{2,1,0:T(8,128)(2,1)S(1)} %collective-permute-done.11.refs_12_), channel_id=1, source_target_pairs={{0,64},{8,24},{16,80},{24,40},{32,96},{40,56},{48,112},{56,8},{64,... | collective-permute-start | bytes 909320 | tf_op jit(solution)/shard_map/ppermute | solution.py:238
  28.6 8.8 %collective-permute-start.5 = (bf16[4,8,4736]{2,1,0:T(8,128)(2,1)S(1)}, bf16[4,8,4736]{2,1,0:T(8,128)(2,1)}, u32[]{:S(2)}, u32[]{:S(2)}) collective-permute-start(bf16[4,8,4736]{2,1,0:T(8,128)(2,1)S(1)} %collective-permute-done.3.refs_4_), channel_id=1, source_target_pairs={{0,192},{8,56},{16,208},{24,8},{32,224},{40,24},{48,240},{56,40},{... | collective-permute-start | bytes 909320 | tf_op jit(solution)/shard_map/ppermute | solution.py:238
  33.1 8.1 %collective-permute-start.8 = (bf16[4,8,4736]{2,1,0:T(8,128)(2,1)S(1)}, bf16[4,8,4736]{2,1,0:T(8,128)(2,1)}, u32[]{:S(2)}, u32[]{:S(2)}) collective-permute-start(bf16[4,8,4736]{2,1,0:T(8,128)(2,1)S(1)} %collective-permute-done.7.refs_8_), channel_id=1, source_target_pairs={{0,64},{8,24},{16,80},{24,40},{32,96},{40,56},{48,112},{56,8},{64,... | collective-permute-start | bytes 909320 | tf_op jit(solution)/shard_map/ppermute | solution.py:238
  37.4 11.2 %collective-permute-start.10 = (bf16[4,8,4736]{2,1,0:T(8,128)(2,1)}, bf16[4,8,4736]{2,1,0:T(8,128)(2,1)}, u32[]{:S(2)}, u32[]{:S(2)}) collective-permute-start(bf16[4,8,4736]{2,1,0:T(8,128)(2,1)} %copy-done.3), channel_id=1, source_target_pairs={{0,192},{8,56},{16,208},{24,8},{32,224},{40,24},{48,240},{56,40},{... | collective-permute-start | bytes 909320 | tf_op jit(solution)/shard_map/ppermute | solution.py:238
  41.2 9.5 %collective-permute-start.14 = (bf16[4,8,4736]{2,1,0:T(8,128)(2,1)}, bf16[4,8,4736]{2,1,0:T(8,128)(2,1)}, u32[]{:S(2)}, u32[]{:S(2)}) collective-permute-start(bf16[4,8,4736]{2,1,0:T(8,128)(2,1)} %copy-done.5), channel_id=1, source_target_pairs={{0,192},{8,56},{16,208},{24,8},{32,224},{40,24},{48,240},{56,40},{... | collective-permute-start | bytes 909320 | tf_op jit(solution)/shard_map/ppermute | solution.py:238
  44.1 8.3 %collective-permute-start.6 = (bf16[4,8,4736]{2,1,0:T(8,128)(2,1)}, bf16[4,8,4736]{2,1,0:T(8,128)(2,1)}, u32[]{:S(2)}, u32[]{:S(2)}) collective-permute-start(bf16[4,8,4736]{2,1,0:T(8,128)(2,1)} %copy-done.7), channel_id=1, source_target_pairs={{0,64},{8,24},{16,80},{24,40},{32,96},{40,56},{48,112},{56,8},{64,... | collective-permute-start | bytes 909320 | tf_op jit(solution)/shard_map/ppermute | solution.py:238
  57.5 15.1 %collective-permute-start.15 = (f32[2,64,512]{2,1,0:T(8,128)S(1)}, f32[2,64,512]{2,1,0:T(8,128)S(1)}, u32[]{:S(2)}, u32[]{:S(2)}) collective-permute-start(f32[2,64,512]{2,1,0:T(8,128)S(1)} %get-tuple-element.27), channel_id=1, source_target_pairs={{0,1},{1,2},{2,3},{3,4},{4,5},{5,6},{6,7},{7,0},{8,9},{9,10},{10,1... | collective-permute-start | bytes 786440 | tf_op jit(solution)/shard_map/ppermute | solution.py:263
  60.7 11.9 %collective-permute-start.16 = (f32[2,64,512]{2,1,0:T(8,128)S(1)}, f32[2,64,512]{2,1,0:T(8,128)S(1)}, u32[]{:S(2)}, u32[]{:S(2)}) collective-permute-start(f32[2,64,512]{2,1,0:T(8,128)S(1)} %get-tuple-element.28), channel_id=1, source_target_pairs={{0,7},{1,0},{2,1},{3,2},{4,3},{5,4},{6,5},{7,6},{8,15},{9,8},{10,9... | collective-permute-start | bytes 786440 | tf_op jit(solution)/shard_map/ppermute | solution.py:263
  69.3 9.3 %collective-permute-start.24 = (f32[2,64,512]{2,1,0:T(8,128)S(1)}, f32[2,64,512]{2,1,0:T(8,128)S(1)}, u32[]{:S(2)}, u32[]{:S(2)}) collective-permute-start(f32[2,64,512]{2,1,0:T(8,128)S(1)} %get-tuple-element.35), channel_id=1, source_target_pairs={{0,1},{1,2},{2,3},{3,4},{4,5},{5,6},{6,7},{7,0},{8,9},{9,10},{10,1... | collective-permute-start | bytes 786440 | tf_op jit(solution)/shard_map/ppermute | solution.py:263
  72.6 9.9 %collective-permute-start.25 = (f32[2,64,512]{2,1,0:T(8,128)S(1)}, f32[2,64,512]{2,1,0:T(8,128)S(1)}, u32[]{:S(2)}, u32[]{:S(2)}) collective-permute-start(f32[2,64,512]{2,1,0:T(8,128)S(1)} %get-tuple-element.36), channel_id=1, source_target_pairs={{0,7},{1,0},{2,1},{3,2},{4,3},{5,4},{6,5},{7,6},{8,15},{9,8},{10,9... | collective-permute-start | bytes 786440 | tf_op jit(solution)/shard_map/ppermute | solution.py:263
  73.2 12.0 %collective-permute-start.17 = (f32[2,64,512]{2,1,0:T(8,128)S(1)}, f32[2,64,512]{2,1,0:T(8,128)S(1)}, u32[]{:S(2)}, u32[]{:S(2)}) collective-permute-start(f32[2,64,512]{2,1,0:T(8,128)S(1)} %get-tuple-element.29), channel_id=1, source_target_pairs={{0,1},{1,2},{2,3},{3,4},{4,5},{5,6},{6,7},{7,0},{8,9},{9,10},{10,1... | collective-permute-start | bytes 786440 | tf_op jit(solution)/shard_map/ppermute | solution.py:263
  76.5 9.3 %collective-permute-start.18 = (f32[2,64,512]{2,1,0:T(8,128)S(1)}, f32[2,64,512]{2,1,0:T(8,128)S(1)}, u32[]{:S(2)}, u32[]{:S(2)}) collective-permute-start(f32[2,64,512]{2,1,0:T(8,128)S(1)} %get-tuple-element.30), channel_id=1, source_target_pairs={{0,7},{1,0},{2,1},{3,2},{4,3},{5,4},{6,5},{7,6},{8,15},{9,8},{10,9... | collective-permute-start | bytes 786440 | tf_op jit(solution)/shard_map/ppermute | solution.py:263
  83.1 10.2 %collective-permute-start.27 = (f32[2,64,512]{2,1,0:T(8,128)S(1)}, f32[2,64,512]{2,1,0:T(8,128)S(1)}, u32[]{:S(2)}, u32[]{:S(2)}) collective-permute-start(f32[2,64,512]{2,1,0:T(8,128)S(1)} %get-tuple-element.38), channel_id=1, source_target_pairs={{0,7},{1,0},{2,1},{3,2},{4,3},{5,4},{6,5},{7,6},{8,15},{9,8},{10,9... | collective-permute-start | bytes 786440 | tf_op jit(solution)/shard_map/ppermute | solution.py:263
  86.4 9.3 %collective-permute-start.19 = (f32[2,64,512]{2,1,0:T(8,128)S(1)}, f32[2,64,512]{2,1,0:T(8,128)S(1)}, u32[]{:S(2)}, u32[]{:S(2)}) collective-permute-start(f32[2,64,512]{2,1,0:T(8,128)S(1)} %get-tuple-element.31), channel_id=1, source_target_pairs={{0,1},{1,2},{2,3},{3,4},{4,5},{5,6},{6,7},{7,0},{8,9},{9,10},{10,1... | collective-permute-start | bytes 786440 | tf_op jit(solution)/shard_map/ppermute | solution.py:263
  93.9 9.6 %collective-permute-start.29 = (f32[2,64,512]{2,1,0:T(8,128)S(1)}, f32[2,64,512]{2,1,0:T(8,128)S(1)}, u32[]{:S(2)}, u32[]{:S(2)}) collective-permute-start(f32[2,64,512]{2,1,0:T(8,128)S(1)} %get-tuple-element.40), channel_id=1, source_target_pairs={{0,7},{1,0},{2,1},{3,2},{4,3},{5,4},{6,5},{7,6},{8,15},{9,8},{10,9... | collective-permute-start | bytes 786440 | tf_op jit(solution)/shard_map/ppermute | solution.py:263
  95.2 11.1 %collective-permute-start.21 = (f32[2,64,512]{2,1,0:T(8,128)S(1)}, f32[2,64,512]{2,1,0:T(8,128)S(1)}, u32[]{:S(2)}, u32[]{:S(2)}) collective-permute-start(f32[2,64,512]{2,1,0:T(8,128)S(1)} %get-tuple-element.32), channel_id=1, source_target_pairs={{0,7},{1,0},{2,1},{3,2},{4,3},{5,4},{6,5},{7,6},{8,15},{9,8},{10,9... | collective-permute-start | bytes 786440 | tf_op jit(solution)/shard_map/ppermute | solution.py:263
  96.3 10.1 %collective-permute-start.20 = (f32[2,64,512]{2,1,0:T(8,128)S(1)}, f32[2,64,512]{2,1,0:T(8,128)S(1)}, u32[]{:S(2)}, u32[]{:S(2)}) collective-permute-start(f32[2,64,512]{2,1,0:T(8,128)S(1)} %add_shares.8), channel_id=1, source_target_pairs={{0,1},{1,2},{2,3},{3,4},{4,5},{5,6},{6,7},{7,0},{8,9},{9,10},{10,1... | collective-permute-start | bytes 786440 | tf_op jit(solution)/shard_map/ppermute | solution.py:263
  (23 other events, 215.4 us)
where the time goes:
time: 126 us
  starting transfers between devices  43.2 us (34%)
  waiting for transfers between devices  43 us (34%)
  Pallas kernels  23.9 us (19%)
  blocking collectives  11.8 us (9%)
  local copies, waits for them, and re-layouts  2.77 us (2%)
    ppermute x15, starting transfers between devices, dp(): return lax.ppermute(array, 'dp', hop(phase, distance))  23.1 us
    ppermute x14, waiting for transfers between devices, send(): return lax.ppermute(array, 'tensor', ring[sign])  22.6 us
    ppermute x15, waiting for transfers between devices, dp(): return lax.ppermute(array, 'dp', hop(phase, distance))  20.3 us
    ppermute x14, starting transfers between devices, send(): return lax.ppermute(array, 'tensor', ring[sign])  19.5 us
    all_to_all x1, blocking collectives, local(): lax.all_to_all(scores, 'dp', split_axis=0, concat_axis=0, tiled=True, axi...  11.8 us
    pallas_call x2, Pallas kernels, project(): pl.pallas_call(functools.partial(project_kernel, lengths, first), in_spec...  9.86 us
    pallas_call x2, Pallas kernels, hold(): pl.pallas_call(hold_kernel, in_specs=[SMEM] + [HBM] * len(arrays), out_sp...  7.87 us
    pallas_call x6, Pallas kernels, add_shares(): pl.pallas_call(functools.partial(add_kernel, tuple(offsets)), in_specs=[S...  3.55 us
  transfers between devices with their start and end apart: 31, of which 19 were waited for; matrix products, arithmetic and copies ran while one was open for 2% of the time, Pallas kernels for 17%

commit v1 on v0

--- a/solution.py
+++ b/solution.py
@@ -40,11 +40,14 @@
     return [pltpu.with_memory_space_constraint(a, pltpu.VMEM) for a in arrays]
 
 
-def hold_kernel(info, *refs):
-    count = len(refs) // 2
+def hold_kernel(places, info, *refs):
+    count = len(places)
     sems = refs[-1]
     copies = [
-        pltpu.make_async_copy(refs[i], refs[count + i], sems.at[i]) for i in range(count)
+        pltpu.make_async_copy(
+            refs[i] if at is None else refs[i].at[at], refs[count + i], sems.at[i]
+        )
+        for i, at in enumerate(places)
     ]
     for copy in copies:
         copy.start()
@@ -53,24 +56,28 @@
 
 
 def hold(info, *arrays):
-    return pl.pallas_call(
-        hold_kernel,
+    places = tuple(at for _, at in arrays)
+    outs = [
+        jax.ShapeDtypeStruct(a.shape if at is None else a.shape[1:], a.dtype) for a, at in arrays
+    ]
+    return pl.pallas_call(
+        functools.partial(hold_kernel, places),
         in_specs=[SMEM] + [HBM] * len(arrays),
         out_specs=[VMEM] * len(arrays),
-        out_shape=[jax.ShapeDtypeStruct(a.shape, a.dtype) for a in arrays],
+        out_shape=outs,
         scratch_shapes=[pltpu.SemaphoreType.DMA((len(arrays),))],
         cost_estimate=pl.CostEstimate(
-            flops=0, bytes_accessed=4 * sum(a.size for a in arrays), transcendentals=0
+            flops=0, bytes_accessed=4 * sum(a.size for a in outs), transcendentals=0
         ),
         compiler_params=pltpu.CompilerParams(vmem_limit_bytes=2 * MIB),
         name="hold",
-    )(info, *[pltpu.with_memory_space_constraint(a, pltpu.HBM) for a in arrays])
+    )(info, *[pltpu.with_memory_space_constraint(a, pltpu.HBM) for a, _ in arrays])
 
 
 def project_kernel(lengths, first, info, *refs):
-    blocks, (acts, grads, part, own, plus, minus) = refs[:16], refs[16:22]
-    table, table_scalars, sem, rows = refs[22], refs[23], refs[24], refs[25:27]
-    in_width, out_width = acts.shape[-1], grads.shape[-1]
+    blocks, acts, (grads, part, own, plus, minus) = refs[:16], refs[16:18], refs[18:23]
+    table, table_scalars, sem, rows = refs[23], refs[24], refs[25], refs[26:28]
+    in_width, out_width = acts[0].shape[-1], grads.shape[-1]
     shares, seqs = part.shape[0], part.shape[1]
     sources = table.shape[0]
     width = 16 * sources
@@ -90,7 +97,7 @@
     for j in range(seqs):
         chosen = rows[j][...].reshape(width, rows[j].shape[-1])
         side_in = lax.dot_general(
-            acts[j], chosen[:, :in_width], contract, preferred_element_type=jnp.float32
+            acts[j][...], chosen[:, :in_width], contract, preferred_element_type=jnp.float32
         )
         side_out = lax.dot_general(
             grads[j],
@@ -107,13 +114,13 @@
 
 def project(info, first, blocks, acts, grads, shares, lengths):
     sources = 16
-    seqs, tokens, in_width = acts.shape
+    seqs, (tokens, in_width) = len(acts), acts[0].shape
     out_width = grads.shape[-1]
     row_width = blocks[0].shape[-1]
     share = (seqs, tokens // shares, sources * 32)
     return pl.pallas_call(
         functools.partial(project_kernel, lengths, first),
-        in_specs=[SMEM] + [VMEM] * 18,
+        in_specs=[SMEM] + [VMEM] * 19,
         out_specs=[VMEM] * 4,
         scratch_shapes=[
             pltpu.VMEM((sources, 128), jnp.int32),
@@ -130,7 +137,7 @@
         ),
         compiler_params=pltpu.CompilerParams(vmem_limit_bytes=18 * MIB),
         name="project",
-    )(info, *on_chip((*blocks, acts, grads)))
+    )(info, *on_chip((*blocks, *acts, grads)))
 
 
 def add_kernel(offsets, info, part, *refs):
@@ -182,24 +189,24 @@
     )(info, *on_chip(terms))
 
 
-def choose_kernel(where, returned, out):
+def choose_kernel(where, returned, out, rows):
     queries, count, tokens = out.shape
+    lines = returned.shape[0]
+    rows[:lines] = returned[:, :tokens]
+    rows[lines:] = returned[:, tokens:]
     for q in range(queries):
         for c in range(count):
-            at = where[HEAD + q * count + c]
-            line = returned[at // 2]
-            slot = at % 2
-            line = jnp.where(slot == 0, line[:tokens], line[tokens:])
-            out[q, c, :] = line
+            out[q, c, :] = rows[where[HEAD + q * count + c]]
 
 
 def choose(where, returned, queries, count):
-    _, width = returned.shape
+    lines, width = returned.shape
     return pl.pallas_call(
         choose_kernel,
         in_specs=[SMEM, VMEM],
         out_specs=VMEM,
         out_shape=jax.ShapeDtypeStruct((queries, count, width // 2), jnp.float32),
+        scratch_shapes=[pltpu.VMEM((2 * lines, width // 2), jnp.float32)],
         compiler_params=pltpu.CompilerParams(vmem_limit_bytes=4 * MIB),
         name="choose",
     )(where, *on_chip([returned]))
@@ -217,8 +224,10 @@
     other_acts = lax.ppermute(activations, "dp", PARTNER)
     other_grads = lax.ppermute(gradients, "dp", PARTNER)
 
-    target_rows = jnp.take(sequence_place, candidates, axis=0)
     positions = jnp.arange(total, dtype=jnp.int32)
+    target_rows = jnp.sum(
+        jnp.where(candidates[:, :, None] == positions, sequence_place, 0), axis=2
+    )
     listed = jnp.any(target_rows[:, :, None] == positions, axis=1)
     number = jnp.arange(queries, dtype=jnp.int32)[:, None]
     flags = listed.astype(jnp.int32)
@@ -252,7 +261,7 @@
     col = (x + jnp.where(core == 0, first_axis, second_axis)) % SIDE
     slot = jnp.sum(jnp.where(target_rows[:, :, None] == positions, before[:, None, :], 0), axis=2)
     kind = jnp.where((target_rows // 2) % 2 == core, 0, 2) + target_rows % 2
-    where = ((target_rows // 4) * 4 + kind) * 2 + slot
+    where = slot * total + (target_rows // 4) * 4 + kind
     heads = jnp.stack([z, 2 * device, 2 * (device ^ 1)])
     info = jnp.concatenate([heads, row * SIDE + col, where.reshape(-1)]).astype(jnp.int32)
 
@@ -262,8 +271,11 @@
     def send(array, sign):
         return lax.ppermute(array, "tensor", ring[sign])
 
-    held_a = hold(info, activations, gradients)
-    held_b = (*hold(info, other_acts), other_grads)
+    (one,) = hold(info, (activations, 0))
+    two, held_grads = hold(info, (activations, 1), (gradients, None))
+    other_one, other_two = hold(info, (other_acts, 0), (other_acts, 1))
+    held_a = ((one, two), held_grads)
+    held_b = ((other_one, other_two), other_grads)
     far_a, far_b = shares // 2, shares - 1 - shares // 2
     streams = []
     for base, held, lengths in ((1, held_a, (far_a, far_b)), (2, held_b, (far_b, far_a))):

time: 126 us -> 128 us (1.016)
  waiting for transfers between devices: 43 us -> 40.2 us
  other arithmetic: 1.25 us -> 3.11 us
  Pallas kernels: 23.9 us -> 25.6 us
  local copies, waits for them, and re-layouts: 2.77 us -> 1.09 us
  blocking collectives: 11.8 us -> 13.2 us
    ppermute x15, waiting for transfers between devices: 20.3 us -> 17.1 us  [dp(): return lax.ppermute(array, 'dp', hop(phase, distance))]
    pallas_call x2 -> x3, Pallas kernels: 7.87 us -> 9.58 us  [hold(): pl.pallas_call(functools.partial(hold_kernel, places), in_specs=[SMEM] +...]
    all_to_all x1, blocking collectives: 11.8 us -> 13.2 us  [local(): lax.all_to_all(scores, 'dp', split_axis=0, concat_axis=0, tiled=True, axi...]
  transfers between devices with their start and end apart: 31 -> 31, of which waited for: 19 -> 18; matrix products, arithmetic and copies ran while one was open for 2% -> 3% of each run, Pallas kernels for 17% -> 18%
where the time goes in v1:
time: 128 us; the launch traced here: 127 us
  starting transfers between devices  43.8 us (34%)
  waiting for transfers between devices  40.2 us (31%)
  Pallas kernels  25.6 us (20%)
  blocking collectives  13.2 us (10%)
  other arithmetic  3.11 us (2%)
    ppermute x15, starting transfers between devices, dp(): return lax.ppermute(array, 'dp', hop(phase, distance))  24 us
    ppermute x14, waiting for transfers between devices, send(): return lax.ppermute(array, 'tensor', ring[sign])  23 us
    ppermute x14, starting transfers between devices, send(): return lax.ppermute(array, 'tensor', ring[sign])  19.3 us
    ppermute x15, waiting for transfers between devices, dp(): return lax.ppermute(array, 'dp', hop(phase, distance))  17.1 us
    all_to_all x1, blocking collectives, local(): lax.all_to_all(scores, 'dp', split_axis=0, concat_axis=0, tiled=True, axi...  13.2 us
    pallas_call x2, Pallas kernels, project(): pl.pallas_call(functools.partial(project_kernel, lengths, first), in_spec...  10.2 us
    pallas_call x3, Pallas kernels, hold(): pl.pallas_call(functools.partial(hold_kernel, places), in_specs=[SMEM] +...  9.58 us
    pallas_call x6, Pallas kernels, add_shares(): pl.pallas_call(functools.partial(add_kernel, tuple(offsets)), in_specs=[S...  3.56 us
  transfers between devices with their start and end apart: 31, of which 18 were waited for; matrix products, arithmetic and copies ran while one was open for 3% of the time, Pallas kernels for 18%

profile of v1, /device:TPU:96, one launch (start us, length us, event | category | flops | bytes accessed | tf_op | source)
XLA Modules:
  0.0 127.3 jit_solution(4103415816114268344)
XLA Ops:
  2.8 2.8 %collective-permute-start.7 = (bf16[4,8,4736]{2,1,0:T(8,128)(2,1)S(1)}, bf16[4,8,4736]{2,1,0:T(8,128)(2,1)S(1)}, u32[]{:S(2)}, u32[]{:S(2)}) collective-permute-start(bf16[4,8,4736]{2,1,0:T(8,128)(2,1)S(1)} %maximum_maximum_fusion.refs_0_), channel_id=1, source_target_pairs={{0,48},{8,200},{16,0},{24,216},{32,16},{40,232},{48,32},{56,248},{... | collective-permute-start | bytes 909320 | tf_op jit(solution)/shard_map/ppermute | solution.py:247
  7.3 5.9 %collective-permute-done.7.refs_8_ = bf16[4,8,4736]{2,1,0:T(8,128)(2,1)S(1)} collective-permute-done((bf16[4,8,4736]{2,1,0:T(8,128)(2,1)S(1)}, bf16[4,8,4736]{2,1,0:T(8,128)(2,1)S(1)}, u32[]{:S(2)}, u32[]{:S(2)}) %collective-permute-start.7) | collective-permute-done | bytes 303136 | tf_op jit(solution)/shard_map/ppermute | solution.py:247
  13.3 3.0 %collective-permute-start.1 = (bf16[4,8,4736]{2,1,0:T(8,128)(2,1)S(1)}, bf16[4,8,4736]{2,1,0:T(8,128)(2,1)S(1)}, u32[]{:S(2)}, u32[]{:S(2)}) collective-permute-start(bf16[4,8,4736]{2,1,0:T(8,128)(2,1)S(1)} %maximum_maximum_fusion.refs_0_), channel_id=1, source_target_pairs={{0,192},{8,56},{16,208},{24,8},{32,224},{40,24},{48,240},{56,40},{... | collective-permute-start | bytes 909320 | tf_op jit(solution)/shard_map/ppermute | solution.py:247
  17.2 3.0 %collective-permute-start.9 = (bf16[4,8,4736]{2,1,0:T(8,128)(2,1)S(1)}, bf16[4,8,4736]{2,1,0:T(8,128)(2,1)S(1)}, u32[]{:S(2)}, u32[]{:S(2)}) collective-permute-start(bf16[4,8,4736]{2,1,0:T(8,128)(2,1)S(1)} %collective-permute-done.7.refs_8_), channel_id=1, source_target_pairs={{0,192},{8,56},{16,208},{24,8},{32,224},{40,24},{48,240},{56,40},{... | collective-permute-start | bytes 909320 | tf_op jit(solution)/shard_map/ppermute | solution.py:247
  20.6 3.7 %collective-permute-start.13 = (bf16[4,8,4736]{2,1,0:T(8,128)(2,1)S(1)}, bf16[4,8,4736]{2,1,0:T(8,128)(2,1)}, u32[]{:S(2)}, u32[]{:S(2)}) collective-permute-start(bf16[4,8,4736]{2,1,0:T(8,128)(2,1)S(1)} %collective-permute-done.11.refs_12_), channel_id=1, source_target_pairs={{0,192},{8,56},{16,208},{24,8},{32,224},{40,24},{48,240},{56,40},{... | collective-permute-start | bytes 909320 | tf_op jit(solution)/shard_map/ppermute | solution.py:247
  25.1 2.2 %collective-permute-start.12 = (bf16[4,8,4736]{2,1,0:T(8,128)(2,1)S(1)}, bf16[4,8,4736]{2,1,0:T(8,128)(2,1)}, u32[]{:S(2)}, u32[]{:S(2)}) collective-permute-start(bf16[4,8,4736]{2,1,0:T(8,128)(2,1)S(1)} %collective-permute-done.11.refs_12_), channel_id=1, source_target_pairs={{0,64},{8,24},{16,80},{24,40},{32,96},{40,56},{48,112},{56,8},{64,... | collective-permute-start | bytes 909320 | tf_op jit(solution)/shard_map/ppermute | solution.py:247
  28.6 3.8 %collective-permute-start.5 = (bf16[4,8,4736]{2,1,0:T(8,128)(2,1)S(1)}, bf16[4,8,4736]{2,1,0:T(8,128)(2,1)}, u32[]{:S(2)}, u32[]{:S(2)}) collective-permute-start(bf16[4,8,4736]{2,1,0:T(8,128)(2,1)S(1)} %collective-permute-done.3.refs_4_), channel_id=1, source_target_pairs={{0,192},{8,56},{16,208},{24,8},{32,224},{40,24},{48,240},{56,40},{... | collective-permute-start | bytes 909320 | tf_op jit(solution)/shard_map/ppermute | solution.py:247
  33.2 3.2 %collective-permute-done.12.refs_13_ = bf16[4,8,4736]{2,1,0:T(8,128)(2,1)} collective-permute-done((bf16[4,8,4736]{2,1,0:T(8,128)(2,1)S(1)}, bf16[4,8,4736]{2,1,0:T(8,128)(2,1)}, u32[]{:S(2)}, u32[]{:S(2)}) %collective-permute-start.12) | collective-permute-done | bytes 303136 | tf_op jit(solution)/shard_map/ppermute | solution.py:247
  36.8 3.8 %collective-permute-start.10 = (bf16[4,8,4736]{2,1,0:T(8,128)(2,1)}, bf16[4,8,4736]{2,1,0:T(8,128)(2,1)}, u32[]{:S(2)}, u32[]{:S(2)}) collective-permute-start(bf16[4,8,4736]{2,1,0:T(8,128)(2,1)} %copy-done.4), channel_id=1, source_target_pairs={{0,192},{8,56},{16,208},{24,8},{32,224},{40,24},{48,240},{56,40},{... | collective-permute-start | bytes 909320 | tf_op jit(solution)/shard_map/ppermute | solution.py:247
  41.3 2.2 %collective-permute-done.2.refs_3_ = bf16[4,8,4736]{2,1,0:T(8,128)(2,1)} collective-permute-done((bf16[4,8,4736]{2,1,0:T(8,128)(2,1)}, bf16[4,8,4736]{2,1,0:T(8,128)(2,1)}, u32[]{:S(2)}, u32[]{:S(2)}) %collective-permute-start.2) | collective-permute-done | bytes 303136 | tf_op jit(solution)/shard_map/ppermute | solution.py:247
  44.4 3.3 %hold.4 = (bf16[512,3584]{1,0:T(8,128)(2,1)S(1)}, bf16[2,512,1024]{2,1,0:T(8,128)(2,1)S(1)}) custom-call(s32[83]{0:T(128)S(1)} %concatenate.6.info.where, bf16[2,512,3584]{2,1,0:T(8,128)(2,1)} %refs_0_.3, bf16[2,512,1024]{2,1,0:T(8,128)(2,1)} %refs_1_.1), custom_call_target="tpu_custom_call" | custom-call | bytes 11534336 | tf_op jit(solution)/shard_map/hold/pallas_call | solution.py:63
  47.7 2.6 %hold.3.refs_16_ = bf16[512,3584]{1,0:T(8,128)(2,1)S(1)} custom-call(s32[83]{0:T(128)S(1)} %concatenate.6.info.where, bf16[2,512,3584]{2,1,0:T(8,128)(2,1)} %refs_0_.3), custom_call_target="tpu_custom_call" | custom-call | bytes 7340032 | tf_op jit(solution)/shard_map/hold/pallas_call | solution.py:63
  51.9 5.1 %project.2 = (f32[8,2,64,512]{3,2,1,0:T(8,128)S(1)}, f32[2,64,512]{2,1,0:T(8,128)S(1)}, f32[2,64,512]{2,1,0:T(8,128)S(1)}, f32[2,64,512]{2,1,0:T(8,128)S(1)}) custom-call(s32[83]{0:T(128)S(1)} %concatenate.6.info.where, bf16[4,8,4736]{2,1,0:T(8,128)(2,1)S(1)} %maximum_maximum_fusion.refs_0_, bf16[4,8,4736]{2,1,0:T(8,128)(2,1)S(1)} %copy-done.3, ...), custom_call_target="tpu_custom_call" | custom-call | flops 2415919104 | bytes 14155776 | tf_op jit(solution)/shard_map/project/pallas_call | solution.py:121
  57.0 3.2 %collective-permute-start.15 = (f32[2,64,512]{2,1,0:T(8,128)S(1)}, f32[2,64,512]{2,1,0:T(8,128)S(1)}, u32[]{:S(2)}, u32[]{:S(2)}) collective-permute-start(f32[2,64,512]{2,1,0:T(8,128)S(1)} %get-tuple-element.29), channel_id=1, source_target_pairs={{0,1},{1,2},{2,3},{3,4},{4,5},{5,6},{6,7},{7,0},{8,9},{9,10},{10,1... | collective-permute-start | bytes 786440 | tf_op jit(solution)/shard_map/ppermute | solution.py:272
  60.2 3.7 %hold.5 = (bf16[512,3584]{1,0:T(8,128)(2,1)S(1)}, bf16[512,3584]{1,0:T(8,128)(2,1)S(1)}) custom-call(s32[83]{0:T(128)S(1)} %concatenate.6.info.where, bf16[2,512,3584]{2,1,0:T(8,128)(2,1)} %collective-permute-done.22.refs_0_.refs_1_, bf16[2,512,3584]{2,1,0:T(8,128)(2,1)} %collective-permute-done.22.refs_0_.refs_1_), custom_call_target="tpu_custom_call" | custom-call | bytes 14680064 | tf_op jit(solution)/shard_map/hold/pallas_call | solution.py:63
  64.0 5.1 %project.3 = (f32[8,2,64,512]{3,2,1,0:T(8,128)S(1)}, f32[2,64,512]{2,1,0:T(8,128)S(1)}, f32[2,64,512]{2,1,0:T(8,128)S(1)}, f32[2,64,512]{2,1,0:T(8,128)S(1)}) custom-call(s32[83]{0:T(128)S(1)} %concatenate.6.info.where, bf16[4,8,4736]{2,1,0:T(8,128)(2,1)S(1)} %maximum_maximum_fusion.refs_0_, bf16[4,8,4736]{2,1,0:T(8,128)(2,1)S(1)} %copy-done.3, ...), custom_call_target="tpu_custom_call" | custom-call | flops 2415919104 | bytes 14155776 | tf_op jit(solution)/shard_map/project/pallas_call | solution.py:121
  69.1 3.3 %collective-permute-start.24 = (f32[2,64,512]{2,1,0:T(8,128)S(1)}, f32[2,64,512]{2,1,0:T(8,128)S(1)}, u32[]{:S(2)}, u32[]{:S(2)}) collective-permute-start(f32[2,64,512]{2,1,0:T(8,128)S(1)} %get-tuple-element.39), channel_id=1, source_target_pairs={{0,1},{1,2},{2,3},{3,4},{4,5},{5,6},{6,7},{7,0},{8,9},{9,10},{10,1... | collective-permute-start | bytes 786440 | tf_op jit(solution)/shard_map/ppermute | solution.py:272
  73.0 3.3 %collective-permute-start.17 = (f32[2,64,512]{2,1,0:T(8,128)S(1)}, f32[2,64,512]{2,1,0:T(8,128)S(1)}, u32[]{:S(2)}, u32[]{:S(2)}) collective-permute-start(f32[2,64,512]{2,1,0:T(8,128)S(1)} %get-tuple-element.31), channel_id=1, source_target_pairs={{0,1},{1,2},{2,3},{3,4},{4,5},{5,6},{6,7},{7,0},{8,9},{9,10},{10,1... | collective-permute-start | bytes 786440 | tf_op jit(solution)/shard_map/ppermute | solution.py:272
  78.4 3.9 %collective-permute-done.25.refs_1_ = f32[2,64,512]{2,1,0:T(8,128)S(1)} collective-permute-done((f32[2,64,512]{2,1,0:T(8,128)S(1)}, f32[2,64,512]{2,1,0:T(8,128)S(1)}, u32[]{:S(2)}, u32[]{:S(2)}) %collective-permute-start.25) | collective-permute-done | bytes 262176 | tf_op jit(solution)/shard_map/ppermute | solution.py:272
  89.9 3.5 %collective-permute-done.27.refs_1_ = f32[2,64,512]{2,1,0:T(8,128)S(1)} collective-permute-done((f32[2,64,512]{2,1,0:T(8,128)S(1)}, f32[2,64,512]{2,1,0:T(8,128)S(1)}, u32[]{:S(2)}, u32[]{:S(2)}) %collective-permute-start.27) | collective-permute-done | bytes 262176 | tf_op jit(solution)/shard_map/ppermute | solution.py:272
  96.1 2.8 %collective-permute-start.20 = (f32[2,64,512]{2,1,0:T(8,128)S(1)}, f32[2,64,512]{2,1,0:T(8,128)S(1)}, u32[]{:S(2)}, u32[]{:S(2)}) collective-permute-start(f32[2,64,512]{2,1,0:T(8,128)S(1)} %add_shares.8), channel_id=1, source_target_pairs={{0,1},{1,2},{2,3},{3,4},{4,5},{5,6},{6,7},{7,0},{8,9},{9,10},{10,1... | collective-permute-start | bytes 786440 | tf_op jit(solution)/shard_map/ppermute | solution.py:272
  99.9 3.6 %collective-permute-done.29.refs_0_ = f32[2,64,512]{2,1,0:T(8,128)S(1)} collective-permute-done((f32[2,64,512]{2,1,0:T(8,128)S(1)}, f32[2,64,512]{2,1,0:T(8,128)S(1)}, u32[]{:S(2)}, u32[]{:S(2)}) %collective-permute-start.29) | collective-permute-done | bytes 262176 | tf_op jit(solution)/shard_map/ppermute | solution.py:272
  106.4 5.4 %collective-permute-done.30.refs_5_ = f32[2,64,512]{2,1,0:T(8,128)S(1)} collective-permute-done((f32[2,64,512]{2,1,0:T(8,128)S(1)}, f32[2,64,512]{2,1,0:T(8,128)S(1)}, u32[]{:S(2)}, u32[]{:S(2)}) %collective-permute-start.30) | collective-permute-done | bytes 262176 | tf_op jit(solution)/shard_map/ppermute | solution.py:272
  112.8 13.2 %all_to_all.5 = f32[16,4,128]{2,1,0:T(4,128)S(1)} all-to-all(f32[16,4,128]{2,1,0:T(4,128)S(1)} %score.1), channel_id=1, replica_groups={{0,16,32,48,64,80,96,112,128,144,160,176,192,208,224,240},{8,24,40,56,7..., dimensions={0} | all-to-all | bytes 65536 | tf_op jit(solution)/shard_map/all_to_all | solution.py:298
  (82 shorter events, 31.2 us)
Async XLA Ops:
  0.0 60.2 %collective-permute-start.22 = (bf16[2,512,3584]{2,1,0:T(8,128)(2,1)}, bf16[2,512,3584]{2,1,0:T(8,128)(2,1)}, u32[]{:S(2)}, u32[]{:S(2)}) collective-permute-start(bf16[2,512,3584]{2,1,0:T(8,128)(2,1)} %refs_0_.3), channel_id=1, source_target_pairs={{0,8},{8,0},{16,24},{24,16},{32,40},{40,32},{48,56},{56,48},{64,72... | collective-permute-start | bytes 22020104 | tf_op jit(solution)/shard_map/ppermute | solution.py:224
  0.0 64.0 %collective-permute-start.23 = (bf16[2,512,1024]{2,1,0:T(8,128)(2,1)}, bf16[2,512,1024]{2,1,0:T(8,128)(2,1)S(1)}, u32[]{:S(2)}, u32[]{:S(2)}) collective-permute-start(bf16[2,512,1024]{2,1,0:T(8,128)(2,1)} %refs_1_.1), channel_id=1, source_target_pairs={{0,8},{8,0},{16,24},{24,16},{32,40},{40,32},{48,56},{56,48},{64,72... | collective-permute-start | bytes 6291464 | tf_op jit(solution)/shard_map/ppermute | solution.py:225
  2.8 10.4 %collective-permute-start.7 = (bf16[4,8,4736]{2,1,0:T(8,128)(2,1)S(1)}, bf16[4,8,4736]{2,1,0:T(8,128)(2,1)S(1)}, u32[]{:S(2)}, u32[]{:S(2)}) collective-permute-start(bf16[4,8,4736]{2,1,0:T(8,128)(2,1)S(1)} %maximum_maximum_fusion.refs_0_), channel_id=1, source_target_pairs={{0,48},{8,200},{16,0},{24,216},{32,16},{40,232},{48,32},{56,248},{... | collective-permute-start | bytes 909320 | tf_op jit(solution)/shard_map/ppermute | solution.py:247
  5.7 10.6 %collective-permute-start.11 = (bf16[4,8,4736]{2,1,0:T(8,128)(2,1)S(1)}, bf16[4,8,4736]{2,1,0:T(8,128)(2,1)S(1)}, u32[]{:S(2)}, u32[]{:S(2)}) collective-permute-start(bf16[4,8,4736]{2,1,0:T(8,128)(2,1)S(1)} %maximum_maximum_fusion.refs_0_), channel_id=1, source_target_pairs={{0,32},{8,136},{16,48},{24,152},{32,0},{40,168},{48,16},{56,184},{... | collective-permute-start | bytes 909320 | tf_op jit(solution)/shard_map/ppermute | solution.py:247
  6.5 10.8 %collective-permute-start.3 = (bf16[4,8,4736]{2,1,0:T(8,128)(2,1)S(1)}, bf16[4,8,4736]{2,1,0:T(8,128)(2,1)S(1)}, u32[]{:S(2)}, u32[]{:S(2)}) collective-permute-start(bf16[4,8,4736]{2,1,0:T(8,128)(2,1)S(1)} %maximum_maximum_fusion.refs_0_), channel_id=1, source_target_pairs={{0,16},{8,72},{16,32},{24,88},{32,48},{40,104},{48,0},{56,120},{64... | collective-permute-start | bytes 909320 | tf_op jit(solution)/shard_map/ppermute | solution.py:247
  16.3 8.0 %collective-permute-start = (bf16[4,8,4736]{2,1,0:T(8,128)(2,1)S(1)}, bf16[4,8,4736]{2,1,0:T(8,128)(2,1)S(1)}, u32[]{:S(2)}, u32[]{:S(2)}) collective-permute-start(bf16[4,8,4736]{2,1,0:T(8,128)(2,1)S(1)} %maximum_maximum_fusion.refs_0_), channel_id=1, source_target_pairs={{0,64},{8,24},{16,80},{24,40},{32,96},{40,56},{48,112},{56,8},{64,... | collective-permute-start | bytes 909320 | tf_op jit(solution)/shard_map/ppermute | solution.py:247
  25.0 8.1 %collective-permute-start.4 = (bf16[4,8,4736]{2,1,0:T(8,128)(2,1)S(1)}, bf16[4,8,4736]{2,1,0:T(8,128)(2,1)}, u32[]{:S(2)}, u32[]{:S(2)}) collective-permute-start(bf16[4,8,4736]{2,1,0:T(8,128)(2,1)S(1)} %collective-permute-done.3.refs_4_), channel_id=1, source_target_pairs={{0,64},{8,24},{16,80},{24,40},{32,96},{40,56},{48,112},{56,8},{64,... | collective-permute-start | bytes 909320 | tf_op jit(solution)/shard_map/ppermute | solution.py:247
  25.1 11.4 %collective-permute-start.12 = (bf16[4,8,4736]{2,1,0:T(8,128)(2,1)S(1)}, bf16[4,8,4736]{2,1,0:T(8,128)(2,1)}, u32[]{:S(2)}, u32[]{:S(2)}) collective-permute-start(bf16[4,8,4736]{2,1,0:T(8,128)(2,1)S(1)} %collective-permute-done.11.refs_12_), channel_id=1, source_target_pairs={{0,64},{8,24},{16,80},{24,40},{32,96},{40,56},{48,112},{56,8},{64,... | collective-permute-start | bytes 909320 | tf_op jit(solution)/shard_map/ppermute | solution.py:247
  28.6 8.1 %collective-permute-start.5 = (bf16[4,8,4736]{2,1,0:T(8,128)(2,1)S(1)}, bf16[4,8,4736]{2,1,0:T(8,128)(2,1)}, u32[]{:S(2)}, u32[]{:S(2)}) collective-permute-start(bf16[4,8,4736]{2,1,0:T(8,128)(2,1)S(1)} %collective-permute-done.3.refs_4_), channel_id=1, source_target_pairs={{0,192},{8,56},{16,208},{24,8},{32,224},{40,24},{48,240},{56,40},{... | collective-permute-start | bytes 909320 | tf_op jit(solution)/shard_map/ppermute | solution.py:247
  33.2 8.1 %collective-permute-start.8 = (bf16[4,8,4736]{2,1,0:T(8,128)(2,1)S(1)}, bf16[4,8,4736]{2,1,0:T(8,128)(2,1)}, u32[]{:S(2)}, u32[]{:S(2)}) collective-permute-start(bf16[4,8,4736]{2,1,0:T(8,128)(2,1)S(1)} %collective-permute-done.7.refs_8_), channel_id=1, source_target_pairs={{0,64},{8,24},{16,80},{24,40},{32,96},{40,56},{48,112},{56,8},{64,... | collective-permute-start | bytes 909320 | tf_op jit(solution)/shard_map/ppermute | solution.py:247
  36.8 13.5 %collective-permute-start.10 = (bf16[4,8,4736]{2,1,0:T(8,128)(2,1)}, bf16[4,8,4736]{2,1,0:T(8,128)(2,1)}, u32[]{:S(2)}, u32[]{:S(2)}) collective-permute-start(bf16[4,8,4736]{2,1,0:T(8,128)(2,1)} %copy-done.4), channel_id=1, source_target_pairs={{0,192},{8,56},{16,208},{24,8},{32,224},{40,24},{48,240},{56,40},{... | collective-permute-start | bytes 909320 | tf_op jit(solution)/shard_map/ppermute | solution.py:247
  41.3 9.0 %collective-permute-start.14 = (bf16[4,8,4736]{2,1,0:T(8,128)(2,1)}, bf16[4,8,4736]{2,1,0:T(8,128)(2,1)}, u32[]{:S(2)}, u32[]{:S(2)}) collective-permute-start(bf16[4,8,4736]{2,1,0:T(8,128)(2,1)} %collective-permute-done.13.refs_14_), channel_id=1, source_target_pairs={{0,192},{8,56},{16,208},{24,8},{32,224},{40,24},{48,240},{56,40},{... | collective-permute-start | bytes 909320 | tf_op jit(solution)/shard_map/ppermute | solution.py:247
  43.5 8.3 %collective-permute-start.6 = (bf16[4,8,4736]{2,1,0:T(8,128)(2,1)}, bf16[4,8,4736]{2,1,0:T(8,128)(2,1)}, u32[]{:S(2)}, u32[]{:S(2)}) collective-permute-start(bf16[4,8,4736]{2,1,0:T(8,128)(2,1)} %collective-permute-done.4.refs_5_), channel_id=1, source_target_pairs={{0,64},{8,24},{16,80},{24,40},{32,96},{40,56},{48,112},{56,8},{64,... | collective-permute-start | bytes 909320 | tf_op jit(solution)/shard_map/ppermute | solution.py:247
  57.0 15.4 %collective-permute-start.15 = (f32[2,64,512]{2,1,0:T(8,128)S(1)}, f32[2,64,512]{2,1,0:T(8,128)S(1)}, u32[]{:S(2)}, u32[]{:S(2)}) collective-permute-start(f32[2,64,512]{2,1,0:T(8,128)S(1)} %get-tuple-element.29), channel_id=1, source_target_pairs={{0,1},{1,2},{2,3},{3,4},{4,5},{5,6},{6,7},{7,0},{8,9},{9,10},{10,1... | collective-permute-start | bytes 786440 | tf_op jit(solution)/shard_map/ppermute | solution.py:272
  60.2 12.2 %collective-permute-start.16 = (f32[2,64,512]{2,1,0:T(8,128)S(1)}, f32[2,64,512]{2,1,0:T(8,128)S(1)}, u32[]{:S(2)}, u32[]{:S(2)}) collective-permute-start(f32[2,64,512]{2,1,0:T(8,128)S(1)} %get-tuple-element.30), channel_id=1, source_target_pairs={{0,7},{1,0},{2,1},{3,2},{4,3},{5,4},{6,5},{7,6},{8,15},{9,8},{10,9... | collective-permute-start | bytes 786440 | tf_op jit(solution)/shard_map/ppermute | solution.py:272
  69.1 9.3 %collective-permute-start.24 = (f32[2,64,512]{2,1,0:T(8,128)S(1)}, f32[2,64,512]{2,1,0:T(8,128)S(1)}, u32[]{:S(2)}, u32[]{:S(2)}) collective-permute-start(f32[2,64,512]{2,1,0:T(8,128)S(1)} %get-tuple-element.39), channel_id=1, source_target_pairs={{0,1},{1,2},{2,3},{3,4},{4,5},{5,6},{6,7},{7,0},{8,9},{9,10},{10,1... | collective-permute-start | bytes 786440 | tf_op jit(solution)/shard_map/ppermute | solution.py:272
  72.4 9.9 %collective-permute-start.25 = (f32[2,64,512]{2,1,0:T(8,128)S(1)}, f32[2,64,512]{2,1,0:T(8,128)S(1)}, u32[]{:S(2)}, u32[]{:S(2)}) collective-permute-start(f32[2,64,512]{2,1,0:T(8,128)S(1)} %get-tuple-element.40), channel_id=1, source_target_pairs={{0,7},{1,0},{2,1},{3,2},{4,3},{5,4},{6,5},{7,6},{8,15},{9,8},{10,9... | collective-permute-start | bytes 786440 | tf_op jit(solution)/shard_map/ppermute | solution.py:272
  73.0 12.0 %collective-permute-start.17 = (f32[2,64,512]{2,1,0:T(8,128)S(1)}, f32[2,64,512]{2,1,0:T(8,128)S(1)}, u32[]{:S(2)}, u32[]{:S(2)}) collective-permute-start(f32[2,64,512]{2,1,0:T(8,128)S(1)} %get-tuple-element.31), channel_id=1, source_target_pairs={{0,1},{1,2},{2,3},{3,4},{4,5},{5,6},{6,7},{7,0},{8,9},{9,10},{10,1... | collective-permute-start | bytes 786440 | tf_op jit(solution)/shard_map/ppermute | solution.py:272
  76.3 9.3 %collective-permute-start.18 = (f32[2,64,512]{2,1,0:T(8,128)S(1)}, f32[2,64,512]{2,1,0:T(8,128)S(1)}, u32[]{:S(2)}, u32[]{:S(2)}) collective-permute-start(f32[2,64,512]{2,1,0:T(8,128)S(1)} %get-tuple-element.32), channel_id=1, source_target_pairs={{0,7},{1,0},{2,1},{3,2},{4,3},{5,4},{6,5},{7,6},{8,15},{9,8},{10,9... | collective-permute-start | bytes 786440 | tf_op jit(solution)/shard_map/ppermute | solution.py:272
  83.0 10.4 %collective-permute-start.27 = (f32[2,64,512]{2,1,0:T(8,128)S(1)}, f32[2,64,512]{2,1,0:T(8,128)S(1)}, u32[]{:S(2)}, u32[]{:S(2)}) collective-permute-start(f32[2,64,512]{2,1,0:T(8,128)S(1)} %get-tuple-element.42), channel_id=1, source_target_pairs={{0,7},{1,0},{2,1},{3,2},{4,3},{5,4},{6,5},{7,6},{8,15},{9,8},{10,9... | collective-permute-start | bytes 786440 | tf_op jit(solution)/shard_map/ppermute | solution.py:272
  86.2 9.3 %collective-permute-start.19 = (f32[2,64,512]{2,1,0:T(8,128)S(1)}, f32[2,64,512]{2,1,0:T(8,128)S(1)}, u32[]{:S(2)}, u32[]{:S(2)}) collective-permute-start(f32[2,64,512]{2,1,0:T(8,128)S(1)} %get-tuple-element.33), channel_id=1, source_target_pairs={{0,1},{1,2},{2,3},{3,4},{4,5},{5,6},{6,7},{7,0},{8,9},{9,10},{10,1... | collective-permute-start | bytes 786440 | tf_op jit(solution)/shard_map/ppermute | solution.py:272
  93.9 9.6 %collective-permute-start.29 = (f32[2,64,512]{2,1,0:T(8,128)S(1)}, f32[2,64,512]{2,1,0:T(8,128)S(1)}, u32[]{:S(2)}, u32[]{:S(2)}) collective-permute-start(f32[2,64,512]{2,1,0:T(8,128)S(1)} %get-tuple-element.44), channel_id=1, source_target_pairs={{0,7},{1,0},{2,1},{3,2},{4,3},{5,4},{6,5},{7,6},{8,15},{9,8},{10,9... | collective-permute-start | bytes 786440 | tf_op jit(solution)/shard_map/ppermute | solution.py:272
  94.8 11.5 %collective-permute-start.21 = (f32[2,64,512]{2,1,0:T(8,128)S(1)}, f32[2,64,512]{2,1,0:T(8,128)S(1)}, u32[]{:S(2)}, u32[]{:S(2)}) collective-permute-start(f32[2,64,512]{2,1,0:T(8,128)S(1)} %get-tuple-element.34), channel_id=1, source_target_pairs={{0,7},{1,0},{2,1},{3,2},{4,3},{5,4},{6,5},{7,6},{8,15},{9,8},{10,9... | collective-permute-start | bytes 786440 | tf_op jit(solution)/shard_map/ppermute | solution.py:272
  96.1 10.3 %collective-permute-start.20 = (f32[2,64,512]{2,1,0:T(8,128)S(1)}, f32[2,64,512]{2,1,0:T(8,128)S(1)}, u32[]{:S(2)}, u32[]{:S(2)}) collective-permute-start(f32[2,64,512]{2,1,0:T(8,128)S(1)} %add_shares.8), channel_id=1, source_target_pairs={{0,1},{1,2},{2,3},{3,4},{4,5},{5,6},{6,7},{7,0},{8,9},{9,10},{10,1... | collective-permute-start | bytes 786440 | tf_op jit(solution)/shard_map/ppermute | solution.py:272
  (13 other events, 72.4 us)
